TPU v7x, 32 devices: a whole 2x2x4 slice. The times are simulated.
32 devices in a mesh: inl: 4 (over x, core), xl: 8 (over z, y).
Axes of the slice: x: 2, y: 2, z: 4, core: 2. Of those that a mesh axis runs over, the one named last changes fastest.
Arguments:
- baseline: float32 [16, 128, 1024], P('inl', 'xl'), may hold values from -600 to 600
- monitor: float32 [16, 128, 1024], P('inl', 'xl'), may hold values from -900 to 900
- shift_model: float32 [4, 32, 128], P(None, None, 'xl'), may hold values from -4 to 4
- knot_start: int32 [32, 4], replicated, may hold values from -12 to 13, as said below
- half_width: int32 [8], P('xl'), may hold values from 1 to 3
Outputs:
- shift_obs: float32 [16, 128, 1024], P('inl', 'xl')
- delta: float32 [4, 32, 128], P(None, 'xl', 'inl')
Inputs may be any that keep to these rules, and one draw needn't show every extreme that they name: `knot_start`: basis function k of a window starts at sample k * 8 - 3 * 4 or one later, relative to the window's first sample.
All inputs are finite; a program needn't handle non-finite values.
Results may differ from a plain program's by a relative error of at most 0.00018.
Values sent between devices are 32-bit elements; how exact they have to be, the bound alone decides.
A program may use at most 64 MiB of HBM per device.

v0:
```python
import jax
import jax.numpy as jnp
from jax import lax
from jax.sharding import PartitionSpec as P

LAGS = 15
TWIN = 12
HMAX = 3
WINLEN = 32
KW = 4
KSTEP = 8


EPSILON = 1e-06
SHARPNESS = 6.0
DAMPING = 0.5


def extended(block, sides, width):
    for axis, dim in sides:
        count = lax.axis_size(axis)
        forward = [(i, i + 1) for i in range(count - 1)]
        backward = [(target, source) for source, target in forward]
        low = lax.ppermute(
            lax.slice_in_dim(block, block.shape[dim] - width, None, axis=dim), axis, forward
        )
        high = lax.ppermute(lax.slice_in_dim(block, 0, width, axis=dim), axis, backward)
        block = jnp.concatenate([low, block, high], axis=dim)
    return block


def spline(offset):
    square = offset * offset
    cubed = square * offset
    piece_one = cubed / 6.0
    piece_two = (-3.0 * cubed + 12.0 * square - 12.0 * offset + 4.0) / 6.0
    piece_three = (3.0 * cubed - 24.0 * square + 60.0 * offset - 44.0) / 6.0
    remain = 4.0 - offset
    piece_four = remain * remain * remain / 6.0
    result = jnp.where(offset < 4.0, piece_four, 0.0 * offset)
    result = jnp.where(offset < 3.0, piece_three, result)
    result = jnp.where(offset < 2.0, piece_two, result)
    result = jnp.where(offset < 1.0, piece_one, result)
    return jnp.where(offset < 0.0, 0.0 * offset, result)


def basis_table(knot_start):
    positions = jnp.arange(WINLEN).astype(jnp.float32)
    offset = (positions[None, None, :] - knot_start[:, :, None].astype(jnp.float32)) / KSTEP
    return spline(offset)


def solve_small(matrix, target):
    lower = [[None] * KW for _ in range(KW)]
    for column in range(KW):
        pivot = matrix[column][column]
        for inner in range(column):
            pivot = pivot - lower[column][inner] * lower[column][inner]
        lower[column][column] = jnp.sqrt(pivot)
        for target_row in range(column + 1, KW):
            entry = matrix[target_row][column]
            for inner in range(column):
                entry = entry - lower[target_row][inner] * lower[column][inner]
            lower[target_row][column] = entry / lower[column][column]
    forward = []
    for column in range(KW):
        entry = target[column]
        for inner in range(column):
            entry = entry - lower[column][inner] * forward[inner]
        forward.append(entry / lower[column][column])
    backward = [None] * KW
    for column in range(KW - 1, -1, -1):
        entry = forward[column]
        for inner in range(column + 1, KW):
            entry = entry - lower[inner][column] * backward[inner]
        backward[column] = entry / lower[column][column]
    return jnp.stack(backward)


def box_time(values):
    samples = values.shape[2]
    width = 2 * TWIN + 1
    padded = jnp.pad(values, ((0, 0), (0, 0), (TWIN, TWIN)))
    partial_sums = {1: padded}
    length = 1
    while 2 * length <= width:
        previous = partial_sums[length]
        partial_sums[2 * length] = previous[:, :, :-length] + previous[:, :, length:]
        length = 2 * length
    total = None
    begin = 0
    remain = width
    while remain > 0:
        if length <= remain:
            piece = partial_sums[length][:, :, begin : begin + samples]
            total = piece if total is None else total + piece
            begin = begin + length
            remain = remain - length
        length = length // 2
    return total


def normal_terms(resid_four, conf_four, table):
    row_count = resid_four.shape[0]
    windows = resid_four.shape[2]
    crossl = resid_four.shape[1]
    grad = jnp.einsum(
        "ixwu,wku->ikwx", conf_four * resid_four, table, precision=lax.Precision.HIGHEST
    )
    hess = jnp.einsum(
        "ixwu,wku,wju->ikjwx", conf_four, table, table, precision=lax.Precision.HIGHEST
    )
    return jnp.concatenate([grad, hess.reshape(row_count, KW * KW, windows, crossl)], axis=1)


def per_device(baseline, monitor, shift_model, knot_start, half_width):
    inline_rows = baseline.shape[0]
    slab_width = baseline.shape[1]
    samples = baseline.shape[2]
    paired = extended(jnp.stack([baseline, monitor]), (("xl", 2),), HMAX)
    base_ext = paired[0]
    moni_ext = paired[1]
    half_span = half_width[0]
    lateral = [
        (jnp.abs(offset) <= half_span).astype(jnp.float32) for offset in range(-HMAX, HMAX + 1)
    ]

    def smooth(values):
        timed = box_time(values)
        total = None
        for place, offset in enumerate(range(-HMAX, HMAX + 1)):
            term = lateral[place] * timed[:, HMAX + offset : HMAX + offset + slab_width]
            total = term if total is None else total + term
        return total

    energy_base = smooth(base_ext * base_ext)
    moni_pad = jnp.pad(moni_ext, ((0, 0), (0, 0), (LAGS, LAGS)))
    energy_mon = smooth(moni_pad * moni_pad)

    def one_lag(lag_index, running):
        total_exp, total_shift, total_corr = running
        lagged = lax.dynamic_slice_in_dim(moni_pad, lag_index, samples, 2)
        correlation = smooth(base_ext * lagged)
        energy = lax.dynamic_slice_in_dim(energy_mon, lag_index, samples, 2)
        normed = correlation / jnp.sqrt(energy_base * energy + EPSILON)
        weight_exp = jnp.exp(SHARPNESS * normed)
        lag_value = jnp.asarray(lag_index - LAGS, jnp.int32).astype(jnp.float32)
        return (
            total_exp + weight_exp,
            total_shift + lag_value * weight_exp,
            total_corr + normed * weight_exp,
        )

    first_lag = one_lag(0, (0.0 * energy_base, 0.0 * energy_base, 0.0 * energy_base))
    total_exp, total_shift, total_corr = lax.fori_loop(1, 2 * LAGS + 1, one_lag, first_lag)
    shift_obs = total_shift / total_exp
    confidence = 0.5 + 0.5 * total_corr / total_exp
    table = basis_table(knot_start)
    modelled = jnp.einsum(
        "kwx,wku->xwu", shift_model, table, precision=lax.Precision.HIGHEST
    ).reshape(slab_width, samples)
    resid = shift_obs - modelled[None]
    resid_piece = lax.all_to_all(resid, "xl", split_axis=2, concat_axis=1, tiled=True)
    conf_piece = lax.all_to_all(confidence, "xl", split_axis=2, concat_axis=1, tiled=True)
    row_count = resid_piece.shape[0]
    crossl = resid_piece.shape[1]
    owned = resid_piece.shape[2] // WINLEN
    table_own = lax.dynamic_slice_in_dim(table, lax.axis_index("xl") * owned, owned, 0)
    resid_four = resid_piece.reshape(row_count, crossl, owned, WINLEN)
    conf_four = conf_piece.reshape(row_count, crossl, owned, WINLEN)
    per_row = normal_terms(resid_four, conf_four, table_own)
    normal = jnp.sum(per_row, axis=0)
    summed = lax.psum(normal, "inl")
    share = summed.shape[2] // lax.axis_size("inl")
    summed = lax.dynamic_slice_in_dim(summed, lax.axis_index("inl") * share, share, 2)
    damping = DAMPING * inline_rows * lax.axis_size("inl")
    matrix = [
        [
            summed[KW + KW * first_k + second_k] + (damping if first_k == second_k else 0.0)
            for second_k in range(KW)
        ]
        for first_k in range(KW)
    ]
    target = [summed[first_k] for first_k in range(KW)]
    delta = solve_small(matrix, target)
    return (shift_obs, delta)


def solution(mesh):
    in_specs = (P("inl", "xl", None), P("inl", "xl", None), P(None, None, "xl"), P(), P("xl"))
    out_specs = (P("inl", "xl", None), P(None, "xl", "inl"))
    return jax.shard_map(
        per_device, mesh=mesh, in_specs=in_specs, out_specs=out_specs, check_vma=False
    )
```

profile of v0, /device:TPU:0, one launch (start us, length us, event | category | flops | bytes accessed | tf_op | source)
XLA Modules:
  0.0 127.3 jit_solution(12901075774814896960)
XLA Ops:
  0.6 1.2 pad_maximum_fusion.2
  1.9 1.3 %collective-permute-start.1 = (f32[2,4,3,1024]{3,2,1,0:T(4,128)S(1)}, f32[2,4,3,1024]{3,2,1,0:T(4,128)S(1)}, u32[]{:S(2)}, u32[]{:S(2)}) collective-permute-start(f32[2,4,3,1024]{3,2,1,0:T(4,128)S(1)} %get-tuple-element.489), channel_id=1, source_target_pairs={{1,0},{2,1},{3,2},{4,3},{5,4},{6,5},{7,6},{9,8},{10,9},{11,10},{12... | collective-permute-start | bytes 294920 | tf_op jit(solution)/shard_map/ppermute | solution.py:27
  3.2 5.5 %collective-permute-start = (f32[2,4,3,1024]{3,2,1,0:T(4,128)S(1)}, f32[2,4,3,1024]{3,2,1,0:T(4,128)S(1)}, u32[]{:S(2)}, u32[]{:S(2)}) collective-permute-start(f32[2,4,3,1024]{3,2,1,0:T(4,128)S(1)} %get-tuple-element.488), channel_id=1, source_target_pairs={{0,1},{1,2},{2,3},{3,4},{4,5},{5,6},{6,7},{8,9},{9,10},{10,11},{11... | collective-permute-start | bytes 294920 | tf_op jit(solution)/shard_map/ppermute | solution.py:24
  8.7 0.8 copy.41
  9.5 0.7 convert_element_type.72
  10.3 0.8 convolution_bitcast_fusion
  12.0 1.2 collective-permute-done
  14.6 0.5 slice_add_fusion.14
  17.4 0.5 multiply_add_fusion.2
  18.0 56.6 %while.21 = (s32[]{:T(128)}, f32[4,16,1024]{2,1,0:T(8,128)S(1)}, f32[4,16,1024]{2,1,0:T(8,128)S(1)}, f32[4,16,1024]{2,1,0:T(8,128)S(1)}, f32[]{:T(128)}, /*index...) while((s32[]{:T(128)}, f32[4,16,1024]{2,1,0:T(8,128)S(1)}, ...), condition=%wide.region_1.2_spmd, body=%wide.region_0.1_spmd.sunk | while | flops 2143487 | bytes 11726543 | solution.py:155
  19.3 0.4 multiply_add_fusion.6
  21.2 0.4 multiply_add_fusion.6
  23.1 0.4 multiply_add_fusion.6
  25.0 0.4 multiply_add_fusion.6
  26.9 0.4 multiply_add_fusion.6
  28.7 0.4 multiply_add_fusion.6
  30.6 0.4 multiply_add_fusion.6
  32.5 0.4 multiply_add_fusion.6
  34.4 0.4 multiply_add_fusion.6
  36.3 0.4 multiply_add_fusion.6
  38.2 0.4 multiply_add_fusion.6
  40.1 0.4 multiply_add_fusion.6
  42.0 0.4 multiply_add_fusion.6
  43.8 0.4 multiply_add_fusion.6
  45.7 0.4 multiply_add_fusion.6
  47.6 0.4 multiply_add_fusion.6
  49.5 0.4 multiply_add_fusion.6
  51.4 0.4 multiply_add_fusion.6
  53.3 0.4 multiply_add_fusion.6
  55.2 0.4 multiply_add_fusion.6
  57.1 0.4 multiply_add_fusion.6
  58.9 0.4 multiply_add_fusion.6
  60.8 0.4 multiply_add_fusion.6
  62.7 0.4 multiply_add_fusion.6
  64.6 0.4 multiply_add_fusion.6
  66.5 0.4 multiply_add_fusion.6
  68.4 0.4 multiply_add_fusion.6
  70.3 0.4 multiply_add_fusion.6
  72.2 0.4 multiply_add_fusion.6
  74.0 0.4 multiply_add_fusion.6
  74.6 1.7 %copy.36 = f32[4,16,1024]{1,0,2:T(4,128)} copy(f32[4,16,1024]{2,1,0:T(8,128)S(1)} %get-tuple-element.429) | data formatting | bytes 524288 | tf_op jit(solution)/shard_map/while | solution.py:155
  76.3 1.7 %copy.37 = f32[4,16,1024]{1,0,2:T(4,128)} copy(f32[4,16,1024]{2,1,0:T(8,128)S(1)} %get-tuple-element.430) | data formatting | bytes 524288 | tf_op jit(solution)/shard_map/while | solution.py:155
  78.1 0.8 copy.39
  78.9 2.3 %reshape.48 = f32[8,1,8192]{2,1,0:T(1,128)} reshape(f32[1024,4,16]{2,1,0:T(4,128)S(1)} %bitcast.52) | data formatting | bytes 524288
  81.2 6.1 %all-to-all-start = ((f32[8,1,8192]{2,1,0:T(1,128)}), f32[8,1,8192]{2,1,0:T(1,128)S(1)}, u32[]{:S(2)}, u32[]{:S(2)}) async-start(f32[8,1,8192]{2,1,0:T(1,128)} %reshape.48), calls=%async_computation | async-start | bytes 524288 | tf_op jit(solution)/shard_map/all_to_all | solution.py:164
  87.3 4.4 %broadcast_subtract_fusion = (f32[4,16,1024]{1,0,2:T(4,128)}, f32[4,16,1024]{1,0,2:T(4,128)S(1)}) fusion(f32[16,1024]{0,1:T(8,128)S(1)} %bitcast.55, f32[4,16,1024]{1,0,2:T(4,128)} %copy.36, f32[4,16,1024]{1,0,2:T(4,128)} %copy.37), kind=kLoop, calls=%fused_computation.31 | loop fusion | flops 131072 | bytes 1114112 | tf_op jit(solution)/shard_map/sub | solution.py:162
  91.7 3.8 %reshape.50 = f32[8,1,8192]{2,1,0:T(1,128)} reshape(f32[1024,4,16]{2,1,0:T(4,128)} %bitcast.51) | data formatting | bytes 524288
  95.5 0.6 all-to-all-done
  96.1 5.4 %all-to-all-start.1 = ((f32[8,1,8192]{2,1,0:T(1,128)}), f32[8,1,8192]{2,1,0:T(1,128)S(1)}, u32[]{:S(2)}, u32[]{:S(2)}) async-start(f32[8,1,8192]{2,1,0:T(1,128)} %reshape.50), calls=%async_computation.1 | async-start | bytes 524288 | tf_op jit(solution)/shard_map/all_to_all | solution.py:163
  101.7 1.4 %copy.50 = f32[4,16,1024]{2,1,0:T(8,128)} copy(f32[4,16,1024]{1,0,2:T(4,128)S(1)} %get-tuple-element.474) | data formatting | bytes 524288
  103.2 0.5 broadcast.174
  103.7 1.3 reduce
  105.0 1.5 %reshape.49 = f32[1024,4,16]{2,1,0:T(4,128)S(1)} reshape(f32[8,8192]{1,0:T(8,128)S(1)} %reduce) | data formatting | bytes 524288
  106.5 0.8 copy.40
  107.2 0.5 reshape.38
  107.7 1.0 convolution_bitcast_fusion.1
  108.7 1.1 all-to-all-done.1
  109.9 1.3 reduce.1
  111.1 1.5 %reshape.51 = f32[1024,4,16]{2,1,0:T(4,128)S(1)} reshape(f32[8,8192]{1,0:T(8,128)S(1)} %reduce.1) | data formatting | bytes 524288
  112.7 0.8 copy.44
  113.4 0.5 reshape.39
  114.2 1.6 %convolution_bitcast_fusion.2 = f32[4,4,4,128]{3,1,0,2:T(4,128)S(1)} fusion(f32[4,128,4,32]{3,2,1,0:T(4,128)S(1)} %mul.591, f32[32,4,32]{2,1,0:T(4,128)} %copy-done.2, s32[]{:T(128)S(6)} %select_n.40), kind=kOutput, calls=%fused_computation.28 | convolution fusion | flops 3145728 | bytes 303108 | tf_op jit(solution)/shard_map/ixwu,wku->ikwx/dot_general | solution.py:107
  115.9 10.5 %psum.7 = f32[20,4,128]{2,1,0:T(4,128)S(1)} all-reduce(f32[20,4,128]{2,1,0:T(4,128)S(1)} %copy.49), channel_id=1, replica_groups=mesh['inl'=4,'xl'=8] {'inl'}, use_global_device_ids=true, to_apply=%region_3.4 | all-reduce | flops 10240 | bytes 81920 | tf_op jit(solution)/shard_map/psum | solution.py:173
  126.7 0.6 pad_maximum_fusion.3
  (249 shorter events, 48.0 us)
Async XLA Ops:
  0.6 12.6 %copy-start = (f32[4,16,1024]{2,1,0:T(8,128)S(1)}, f32[4,16,1024]{2,1,0:T(8,128)}, u32[]{:S(2)}) copy-start(f32[4,16,1024]{2,1,0:T(8,128)} %param.8) | copy-start | bytes 786436
  0.6 12.6 %copy-start.1 = (f32[4,16,1024]{2,1,0:T(8,128)S(1)}, f32[4,16,1024]{2,1,0:T(8,128)}, u32[]{:S(2)}) copy-start(f32[4,16,1024]{2,1,0:T(8,128)} %param.7) | copy-start | bytes 786436
  1.9 10.1 %collective-permute-start.1 = (f32[2,4,3,1024]{3,2,1,0:T(4,128)S(1)}, f32[2,4,3,1024]{3,2,1,0:T(4,128)S(1)}, u32[]{:S(2)}, u32[]{:S(2)}) collective-permute-start(f32[2,4,3,1024]{3,2,1,0:T(4,128)S(1)} %get-tuple-element.489), channel_id=1, source_target_pairs={{1,0},{2,1},{3,2},{4,3},{5,4},{6,5},{7,6},{9,8},{10,9},{11,10},{12... | collective-permute-start | bytes 294920 | tf_op jit(solution)/shard_map/ppermute | solution.py:27
  3.2 10.0 %collective-permute-start = (f32[2,4,3,1024]{3,2,1,0:T(4,128)S(1)}, f32[2,4,3,1024]{3,2,1,0:T(4,128)S(1)}, u32[]{:S(2)}, u32[]{:S(2)}) collective-permute-start(f32[2,4,3,1024]{3,2,1,0:T(4,128)S(1)} %get-tuple-element.488), channel_id=1, source_target_pairs={{0,1},{1,2},{2,3},{3,4},{4,5},{5,6},{6,7},{8,9},{9,10},{10,11},{11... | collective-permute-start | bytes 294920 | tf_op jit(solution)/shard_map/ppermute | solution.py:24
  81.2 14.9 %all-to-all-start = ((f32[8,1,8192]{2,1,0:T(1,128)}), f32[8,1,8192]{2,1,0:T(1,128)S(1)}, u32[]{:S(2)}, u32[]{:S(2)}) async-start(f32[8,1,8192]{2,1,0:T(1,128)} %reshape.48), calls=%async_computation | async-start | bytes 524288 | tf_op jit(solution)/shard_map/all_to_all | solution.py:164
  96.1 13.8 %all-to-all-start.1 = ((f32[8,1,8192]{2,1,0:T(1,128)}), f32[8,1,8192]{2,1,0:T(1,128)S(1)}, u32[]{:S(2)}, u32[]{:S(2)}) async-start(f32[8,1,8192]{2,1,0:T(1,128)} %reshape.50), calls=%async_computation.1 | async-start | bytes 524288 | tf_op jit(solution)/shard_map/all_to_all | solution.py:163
  101.7 1.5 %copy-start.2 = (f32[32,4,32]{2,1,0:T(4,128)}, f32[32,4,32]{2,1,0:T(4,128)S(1)}, u32[]{:S(2)}) copy-start(f32[32,4,32]{2,1,0:T(4,128)S(1)} %fusion.46) | copy-start | bytes 49156
where the time goes:
time: 128 us; the launch traced here: 127 us
  other arithmetic  63.6 us (50%)
  local copies, waits for them, and re-layouts  24.9 us (19%)
  starting transfers between devices  18.3 us (14%)
  blocking collectives  10.5 us (8%)
  matrix products  3.41 us (3%)
  waiting for transfers between devices  2.93 us (2%)
  loops' own time  2.02 us (2%)
  between operations  1.66 us (1%)
    add x98, other arithmetic, box_time(): previous[:, :, :-length] + previous[:, :, length:]  21.5 us
    add x31, other arithmetic, one_lag(): total_corr + normed * weight_exp  12 us
    unnamed x12, local copies, waits for them, and re-layouts  11.3 us
    psum x1, blocking collectives, per_device(): summed = lax.psum(normal, 'inl')  10.5 us
    add x33, other arithmetic, box_time(): total = piece if total is None else total + piece  9.07 us
    all_to_all x1, starting transfers between devices, per_device(): lax.all_to_all(confidence, 'xl', split_axis=2, concat_axis=1, tiled=True)  6.08 us
    slice x33, local copies, waits for them, and re-layouts, box_time(): previous[:, :, :-length] + previous[:, :, length:]  5.94 us
    ppermute x1, starting transfers between devices, extended(): lax.ppermute(lax.slice_in_dim(block, block.shape[dim] - width, None, axis...  5.51 us
  transfers between devices with their start and end apart: 4, of which 3 were waited for; matrix products, arithmetic and copies ran while one was open for 14% of the time, Pallas kernels for 0%

commit v1 on v0

v1 whole, which is shorter than its diff:
```python
import functools
import math

import jax
import jax.numpy as jnp
from jax import lax
from jax.experimental import pallas as pl
from jax.experimental.pallas import tpu as pltpu
from jax.sharding import PartitionSpec as P

LAGS = 15
TWIN = 12
HMAX = 3
WINLEN = 32
KW = 4
KSTEP = 8
EPSILON = 1e-06
SHARPNESS = 6.0
DAMPING = 0.5

LANES = 128
SUB = 8
REACH = LAGS + TWIN
PAIRS = [(k, j) for k in range(KW) for j in range(k + 1)]
TERMS = KW + len(PAIRS)
MESH_ID = pl.DeviceIdType.MESH


def spline(offset):
    square = offset * offset
    cubed = square * offset
    piece_one = cubed / 6.0
    piece_two = (-3.0 * cubed + 12.0 * square - 12.0 * offset + 4.0) / 6.0
    piece_three = (3.0 * cubed - 24.0 * square + 60.0 * offset - 44.0) / 6.0
    remain = 4.0 - offset
    piece_four = remain * remain * remain / 6.0
    result = jnp.where(offset < 4.0, piece_four, 0.0 * offset)
    result = jnp.where(offset < 3.0, piece_three, result)
    result = jnp.where(offset < 2.0, piece_two, result)
    result = jnp.where(offset < 1.0, piece_one, result)
    return jnp.where(offset < 0.0, 0.0 * offset, result)


def box_sums(term, count, put):
    outs = -(-count // SUB)
    terms = {}

    def block(number):
        if number not in terms:
            terms[number] = [term(number * SUB + j) for j in range(SUB)]
        return terms[number]

    totals = {}
    suffixes = {}

    def total(number):
        if number not in totals:
            vals = block(number)
            while len(vals) > 1:
                vals = [vals[2 * j] + vals[2 * j + 1] for j in range(len(vals) // 2)]
            totals[number] = vals[0]
        return totals[number]

    def suffix(number):
        if number not in suffixes:
            vals = list(block(number))
            for j in range(SUB - 2, -1, -1):
                vals[j] = vals[j] + vals[j + 1]
            suffixes[number] = vals
            totals[number] = vals[0]
        return suffixes[number]

    for number in range(outs):
        tail = suffix(number)
        if number + 1 < outs:
            suffix(number + 1)
        if number + 2 < outs:
            suffix(number + 2)
        run = total(number + 1) + total(number + 2)
        for j in range(SUB):
            if number * SUB + j < count:
                position = (number + 3) * SUB + j
                if number + 3 in terms:
                    value = terms[number + 3][j]
                elif number + 3 < outs + 2:
                    value = block(number + 3)[j]
                else:
                    value = term(position)
                run = run + value
                put(number * SUB + j, tail[j] + run)


def main_kernel(
    half_ref, pair_ref, model_ref, knot_ref, shift_ref, normal_ref,
    base, moni, timed, ebase, emoni, texp, tshift, tcorr, phi, flat,
):
    width = ebase.shape[1]
    rows = base.shape[1]
    half = half_ref[0]
    take_two = (half >= 2).astype(jnp.float32)
    take_three = (half >= 3).astype(jnp.float32)
    lane = lax.broadcasted_iota(jnp.int32, (rows, LANES), 1) % WINLEN
    has_before = (lane != 0).astype(jnp.float32)
    has_after = (lane != WINLEN - 1).astype(jnp.float32)

    for which, (ref, halo) in enumerate(((base, TWIN), (moni, REACH))):
        for u in range(WINLEN):
            value = pair_ref[which, u]
            ref[halo + u] = value
            if u >= WINLEN - halo:
                ref[halo + u - WINLEN] = pltpu.roll(value, 1, 1) * has_before
            if u < halo:
                ref[halo + u + WINLEN] = pltpu.roll(value, LANES - 1, 1) * has_after

    def smooth(term, count, put):
        for part in range(rows // SUB):
            band = pl.ds(part * SUB, SUB)

            def keep(r, value, band=band):
                timed[r, band, :] = value

            box_sums(lambda r, band=band: term(r, band), count, keep)
        for r in range(count):
            for part in range(width // SUB):
                near = [timed[r, pl.ds(part * SUB + d, SUB), :] for d in range(2 * HMAX + 1)]
                value = near[3] + (near[2] + near[4])
                value = value + take_two * (near[1] + near[5])
                value = value + take_three * (near[0] + near[6])
                put(r, pl.ds(part * SUB, SUB), value)

    def base_square(r, band):
        value = base[r, band, :]
        return value * value

    def put_base(r, band, value):
        ebase[r, band, :] = value

    smooth(base_square, WINLEN, put_base)

    def moni_square(r, band):
        value = moni[r, band, :]
        return value * value

    def put_moni(r, band, value):
        emoni[r, band, :] = value

    smooth(moni_square, WINLEN + 2 * LAGS, put_moni)

    texp[...] = jnp.zeros_like(texp)
    tshift[...] = jnp.zeros_like(tshift)
    tcorr[...] = jnp.zeros_like(tcorr)

    @pl.loop(0, 2 * LAGS + 1)
    def _(lag):
        lag_value = (lag - LAGS).astype(jnp.float32)

        def product(r, band):
            return base[r, band, :] * moni[lag + r, band, :]

        def finish(r, band, value):
            energy = ebase[r, band, :] * emoni[lag + r, band, :] + EPSILON
            normed = value * lax.rsqrt(energy)
            weight = jnp.exp2(normed * (SHARPNESS * math.log2(math.e)))
            texp[r, band, :] += weight
            tshift[r, band, :] += lag_value * weight
            tcorr[r, band, :] += normed * weight

        smooth(product, WINLEN, finish)

    sample = lax.broadcasted_iota(jnp.int32, (WINLEN, LANES), 0).astype(jnp.float32)
    for k in range(KW):
        start = knot_ref[pl.ds(k, 1), :].astype(jnp.float32)
        phi[k] = spline((sample - start) / KSTEP)

    for part in range(width // SUB):
        band = pl.ds(part * SUB, SUB)
        sums = [jnp.zeros((SUB, LANES), jnp.float32)] * TERMS
        for u in range(WINLEN):
            inverse = 1.0 / texp[u, band, :]
            observed = tshift[u, band, :] * inverse
            shift_ref[u, band, :] = observed
            conf = 0.5 + 0.5 * (tcorr[u, band, :] * inverse)
            basis = [phi[k, pl.ds(u, 1), :] for k in range(KW)]
            tau = model_ref[0, band, :] * basis[0]
            for k in range(1, KW):
                tau = tau + model_ref[k, band, :] * basis[k]
            weighted = conf * (observed - tau)
            for k in range(KW):
                sums[k] = sums[k] + weighted * basis[k]
            for place, (k, j) in enumerate(PAIRS):
                sums[KW + place] = sums[KW + place] + conf * (basis[k] * basis[j])
        for place in range(TERMS):
            value = sums[place]
            value = value + pltpu.roll(value, 2 * WINLEN, 1)
            value = value + pltpu.roll(value, WINLEN, 1)
            flat[pl.ds(place * width + part * SUB, SUB), :] = value
    spare = flat.shape[0] - TERMS * width
    if spare:
        flat[pl.ds(TERMS * width, spare), :] = jnp.zeros((spare, LANES), jnp.float32)
    turned = flat[...].T
    owners, share = normal_ref.shape[0], normal_ref.shape[1]
    for owner in range(owners):
        normal_ref[owner] = turned[owner * share : (owner + 1) * share]


def solve_small(matrix, target):
    lower = [[None] * KW for _ in range(KW)]
    for column in range(KW):
        pivot = matrix[column][column]
        for inner in range(column):
            pivot = pivot - lower[column][inner] * lower[column][inner]
        lower[column][column] = jnp.sqrt(pivot)
        for target_row in range(column + 1, KW):
            entry = matrix[target_row][column]
            for inner in range(column):
                entry = entry - lower[target_row][inner] * lower[column][inner]
            lower[target_row][column] = entry / lower[column][column]
    forward = []
    for column in range(KW):
        entry = target[column]
        for inner in range(column):
            entry = entry - lower[column][inner] * forward[inner]
        forward.append(entry / lower[column][column])
    backward = [None] * KW
    for column in range(KW - 1, -1, -1):
        entry = forward[column]
        for inner in range(column + 1, KW):
            entry = entry - lower[inner][column] * backward[inner]
        backward[column] = entry / lower[column][column]
    return backward


def owner_kernel(groups, slabs, width, damping, mine_ref, out_ref, held, send_sem, recv_sem):
    row, col = lax.axis_index("inl"), lax.axis_index("xl")
    each = slabs // groups
    target_row = col // each
    place = row * each + col % each
    barrier = pltpu.get_barrier_semaphore()
    for step in range(slabs):
        source_row, source_col = step // each, row * each + step % each

        @pl.when(jnp.logical_or(source_row != row, source_col != col))
        def _():
            pl.semaphore_signal(
                barrier, inc=1, device_id=(source_row, source_col), device_id_type=MESH_ID
            )

    @pl.when(target_row == row)
    def _():
        pl.semaphore_wait(barrier, slabs - 1)

    @pl.when(target_row != row)
    def _():
        pl.semaphore_wait(barrier, slabs)

    def send(step):
        return pltpu.make_async_remote_copy(
            src_ref=mine_ref.at[step],
            dst_ref=held.at[place],
            send_sem=send_sem.at[step],
            recv_sem=recv_sem.at[place],
            device_id=(target_row, step),
            device_id_type=MESH_ID,
        )

    def local():
        return pltpu.make_async_copy(mine_ref.at[col], held.at[place], recv_sem.at[place])

    for step in range(slabs):
        self_copy = jnp.logical_and(target_row == row, col == step)

        @pl.when(self_copy)
        def _():
            local().start()

        @pl.when(jnp.logical_not(self_copy))
        def _():
            send(step).start()

    for step in range(slabs):
        pltpu.make_async_copy(mine_ref.at[0], held.at[step], recv_sem.at[step]).wait()

    share = held.shape[1]
    for part in range(each):
        total = held[part]
        for group in range(1, groups):
            total = total + held[group * each + part]

        def term(number):
            return total[:, number * width : (number + 1) * width]

        matrix = [[None] * KW for _ in range(KW)]
        for number, (k, j) in enumerate(PAIRS):
            matrix[k][j] = term(KW + number) + (damping if k == j else 0.0)
        delta = solve_small(matrix, [term(k) for k in range(KW)])
        for k in range(KW):
            out_ref[k, :, pl.ds(part * width, width)] = delta[k]

    for step in range(slabs):
        self_copy = jnp.logical_and(target_row == row, col == step)

        @pl.when(jnp.logical_not(self_copy))
        def _():
            send(step).wait_send()


def extended(block, axis, dim, width):
    count = lax.axis_size(axis)
    forward = [(i, i + 1) for i in range(count - 1)]
    backward = [(target, source) for source, target in forward]
    low = lax.ppermute(
        lax.slice_in_dim(block, block.shape[dim] - width, None, axis=dim), axis, forward
    )
    high = lax.ppermute(lax.slice_in_dim(block, 0, width, axis=dim), axis, backward)
    return jnp.concatenate([low, block, high], axis=dim)


def per_device(baseline, monitor, shift_model, knot_start, half_width):
    inline_rows, width, samples = baseline.shape
    windows = samples // WINLEN
    groups, slabs = lax.axis_size("inl"), lax.axis_size("xl")
    share = windows // slabs
    rows = -(-(width + 2 * HMAX) // SUB) * SUB
    paired = extended(jnp.stack([baseline, monitor]), "xl", 2, HMAX)
    paired = jnp.pad(paired, ((0, 0), (0, 0), (0, rows - width - 2 * HMAX), (0, 0)))
    pair = paired.reshape(2, inline_rows, rows, windows, WINLEN)
    pair = pair.transpose(0, 4, 2, 1, 3).reshape(2, WINLEN, rows, LANES)
    model = jnp.tile(shift_model.transpose(0, 2, 1), (1, 1, inline_rows))
    knots = jnp.tile(knot_start.T, (1, inline_rows))
    packed = -(-(TERMS * width) // LANES) * LANES
    block = (WINLEN, width, LANES)
    f32 = jnp.float32
    whole = pl.BlockSpec(memory_space=pltpu.VMEM)
    shift, normal = pl.pallas_call(
        main_kernel,
        out_shape=(
            jax.ShapeDtypeStruct(block, f32),
            jax.ShapeDtypeStruct((slabs, share, packed), f32),
        ),
        in_specs=[pl.BlockSpec(memory_space=pltpu.SMEM), whole, whole, whole],
        out_specs=(whole, whole),
        scratch_shapes=[
            pltpu.VMEM((WINLEN + 2 * TWIN, rows, LANES), f32),
            pltpu.VMEM((WINLEN + 2 * REACH + 2, rows, LANES), f32),
            pltpu.VMEM((WINLEN + 2 * LAGS, rows, LANES), f32),
            pltpu.VMEM(block, f32),
            pltpu.VMEM((WINLEN + 2 * LAGS, width, LANES), f32),
            pltpu.VMEM(block, f32),
            pltpu.VMEM(block, f32),
            pltpu.VMEM(block, f32),
            pltpu.VMEM((KW, WINLEN, LANES), f32),
            pltpu.VMEM((packed, LANES), f32),
        ],
        compiler_params=pltpu.CompilerParams(vmem_limit_bytes=32 * 1024 * 1024),
        name="lags",
    )(half_width, pair, model, knots)
    shift_obs = shift.reshape(WINLEN, width, inline_rows, windows)
    shift_obs = shift_obs.transpose(2, 1, 3, 0).reshape(inline_rows, width, samples)
    each = slabs // groups
    delta = pl.pallas_call(
        functools.partial(owner_kernel, groups, slabs, width, DAMPING * inline_rows * groups),
        out_shape=jax.ShapeDtypeStruct((KW, share, each * width), f32),
        in_specs=[whole],
        out_specs=whole,
        scratch_shapes=[
            pltpu.VMEM((slabs, share, packed), f32),
            pltpu.SemaphoreType.DMA((slabs,)),
            pltpu.SemaphoreType.DMA((slabs,)),
        ],
        compiler_params=pltpu.CompilerParams(collective_id=0, has_side_effects=True),
        name="owners",
    )(normal)
    return (shift_obs, delta)


def solution(mesh):
    in_specs = (P("inl", "xl", None), P("inl", "xl", None), P(None, None, "xl"), P(), P("xl"))
    out_specs = (P("inl", "xl", None), P(None, "xl", "inl"))
    return jax.shard_map(
        per_device, mesh=mesh, in_specs=in_specs, out_specs=out_specs, check_vma=False
    )
```

time: 128 us -> 50 us (0.39)
  other arithmetic: 63.6 us -> 3.23 us
  Pallas kernels: 0 us -> 21.2 us
  starting transfers between devices: 18.3 us -> 6.17 us
  blocking collectives: 10.5 us -> 0 us
  local copies, waits for them, and re-layouts: 24.9 us -> 14.4 us
  matrix products: 3.41 us -> 0 us
  loops' own time: 2.02 us -> 0 us
    add x195 -> x0, other arithmetic: 47.6 us -> none  [the longest x98 21.5 us: box_time(): previous[:, :, :-length] + previous[:, :, length:]]
    pallas_call x0 -> x2, Pallas kernels: none -> 21.2 us  [the longest x1 10.6 us: per_device(): pl.pallas_call(functools.partial(owner_kernel, groups, slabs, width, DAMP...]
    all_to_all x2 -> x0, starting transfers between devices: 11.5 us -> none  [the longest x1 6.08 us: per_device(): lax.all_to_all(confidence, 'xl', split_axis=2, concat_axis=1, tiled=True)]
    psum x1 -> x0, blocking collectives: 10.5 us -> none  [per_device(): summed = lax.psum(normal, 'inl')]
    unnamed x12 -> x3, local copies, waits for them, and re-layouts: 11.3 us -> 1.93 us
    reshape x2 -> x5, local copies, waits for them, and re-layouts: 0.9 us -> 10.2 us  [the longest x2 5.73 us: per_device(): pair = paired.reshape(2, inline_rows, rows, windows, WINLEN)]
    slice x33 -> x0, local copies, waits for them, and re-layouts: 5.94 us -> none  [box_time(): previous[:, :, :-length] + previous[:, :, length:]]
    mul x32 -> x0, other arithmetic: 5.64 us -> none  [the longest x30 5.19 us: one_lag(): correlation = smooth(base_ext * lagged)]
  transfers between devices with their start and end apart: 4 -> 2, of which waited for: 3 -> 1; matrix products, arithmetic and copies ran while one was open for 14% -> 3% of each run, Pallas kernels for 0% -> 0%
where the time goes in v1:
time: 50 us; the launch traced here: 49.6 us
  Pallas kernels  21.2 us (42%)
  local copies, waits for them, and re-layouts  14.4 us (29%)
  starting transfers between devices  6.17 us (12%)
  other arithmetic  3.23 us (6%)
  waiting for transfers between devices  3.22 us (6%)
  between operations  1.36 us (3%)
    pallas_call x1, Pallas kernels, per_device(): pl.pallas_call(functools.partial(owner_kernel, groups, slabs, width, DAMP...  10.6 us
    pallas_call x1, Pallas kernels, per_device(): pl.pallas_call(main_kernel, out_shape=(jax.ShapeDtypeStruct(block, f32),...  10.6 us
    reshape x2, local copies, waits for them, and re-layouts, per_device(): pair = paired.reshape(2, inline_rows, rows, windows, WINLEN)  5.73 us
    ppermute x1, starting transfers between devices, extended(): lax.ppermute(lax.slice_in_dim(block, block.shape[dim] - width, None, axis...  4.88 us
    ppermute x1, waiting for transfers between devices, extended(): lax.ppermute(lax.slice_in_dim(block, 0, width, axis=dim), axis, backward)  3.22 us
    reshape x1, local copies, waits for them, and re-layouts, per_device(): pair = pair.transpose(0, 4, 2, 1, 3).reshape(2, WINLEN, rows, LANES)  2.83 us
    concatenate x1, other arithmetic, extended(): return jnp.concatenate([low, block, high], axis=dim)  2.08 us
    unnamed x3, local copies, waits for them, and re-layouts  1.93 us
  transfers between devices with their start and end apart: 2, of which 1 were waited for; matrix products, arithmetic and copies ran while one was open for 3% of the time, Pallas kernels for 0%

profile of v1, /device:TPU:0, one launch (start us, length us, event | category | flops | bytes accessed | tf_op | source)
XLA Modules:
  0.0 49.6 jit_solution(2771935939907851502)
XLA Ops:
  0.6 1.2 %pad_maximum_fusion.1 = (f32[2,4,3,1024]{3,2,1,0:T(4,128)S(1)}, f32[2,4,3,1024]{3,2,1,0:T(4,128)S(1)}) fusion(f32[1,4,16,1024]{3,2,1,0:T(8,128)} %bitcast.12, f32[1,4,16,1024]{3,2,1,0:T(8,128)} %bitcast.14), kind=kLoop, calls=%fused_computation.7 | loop fusion | flops 49152 | bytes 720896 | tf_op jit(solution)/shard_map/slice | solution.py:312
  1.8 4.9 %collective-permute-start = (f32[2,4,3,1024]{3,2,1,0:T(4,128)S(1)}, f32[2,4,3,1024]{3,2,1,0:T(4,128)S(1)}, u32[]{:S(2)}, u32[]{:S(2)}) collective-permute-start(f32[2,4,3,1024]{3,2,1,0:T(4,128)S(1)} %get-tuple-element.6), channel_id=1, source_target_pairs={{0,1},{1,2},{2,3},{3,4},{4,5},{5,6},{6,7},{8,9},{9,10},{10,11},{11... | collective-permute-start | bytes 294920 | tf_op jit(solution)/shard_map/ppermute | solution.py:311
  6.7 1.3 %collective-permute-start.1 = (f32[2,4,3,1024]{3,2,1,0:T(4,128)S(1)}, f32[2,4,3,1024]{3,2,1,0:T(4,128)S(1)}, u32[]{:S(2)}, u32[]{:S(2)}) collective-permute-start(f32[2,4,3,1024]{3,2,1,0:T(4,128)S(1)} %get-tuple-element.7), channel_id=1, source_target_pairs={{1,0},{2,1},{3,2},{4,3},{5,4},{6,5},{7,6},{9,8},{10,9},{11,10},{12... | collective-permute-start | bytes 294920 | tf_op jit(solution)/shard_map/ppermute | solution.py:314
  8.0 0.8 %tile.8 = f32[4,16,4,32]{3,2,1,0:T(4,128)S(1)} broadcast(f32[4,16,32]{2,1,0:T(8,128)} %bitcast.16), dimensions={0,1,3} | broadcast | bytes 40960 | tf_op jit(solution)/shard_map/tile | solution.py:328
  8.8 0.1 tile.9.model_ref
  8.9 0.7 %tile.20 = s32[4,4,32]{2,1,0:T(4,128)S(1)} broadcast(s32[4,32]{1,0:T(4,128)} %bitcast.17), dimensions={0,2} | broadcast | bytes 2560 | tf_op jit(solution)/shard_map/tile | solution.py:329
  9.6 0.1 tile.21.knot_ref
  10.3 0.0 collective-permute-done
  10.3 3.2 %collective-permute-done.1 = f32[2,4,3,1024]{3,2,1,0:T(4,128)S(1)} collective-permute-done((f32[2,4,3,1024]{3,2,1,0:T(4,128)S(1)}, f32[2,4,3,1024]{3,2,1,0:T(4,128)S(1)}, u32[]{:S(2)}, u32[]{:S(2)}) %collective-permute-start.1) | collective-permute-done | bytes 98336 | tf_op jit(solution)/shard_map/ppermute | solution.py:314
  13.5 2.1 %select_maximum_fusion = f32[2,4,24,1024]{3,2,1,0:T(8,128)} fusion(f32[2,4,3,1024]{3,2,1,0:T(4,128)S(1)} %collective-permute-done.1, f32[2,4,3,1024]{3,2,1,0:T(4,128)S(1)} %collective-permute-done, f32[1,4,16,1024]{3,2,1,0:T(8,128)} %bitcast.13, f32[1,4,16,1024]{3,2,1,0:T(8,128)} %bitcast.15), kind=kLoop, calls=%fused_computation | loop fusion | flops 1572864 | bytes 1507328 | tf_op jit(solution)/shard_map/concatenate | solution.py:315
  15.6 2.1 %reshape.24 = f32[2,4,24,32,32]{4,3,2,1,0:T(8,128)S(1)} reshape(f32[2,4,24,1024]{3,2,1,0:T(8,128)} %select_maximum_fusion) | data formatting | bytes 1572864 | tf_op jit(solution)/shard_map/reshape | solution.py:326
  17.7 3.7 %copy.7 = f32[2,4,24,32,32]{3,1,2,4,0:T(4,128)} copy(f32[2,4,24,32,32]{4,3,2,1,0:T(8,128)S(1)} %reshape.24) | data formatting | bytes 1572864 | tf_op jit(solution)/shard_map/reshape | solution.py:326
  21.4 2.8 %reshape.25.pair_ref = f32[2,32,24,128]{3,2,1,0:T(8,128)S(1)} reshape(f32[2,32,24,4,32]{4,3,2,1,0:T(4,128)} %bitcast.10) | data formatting | bytes 1572864 | tf_op jit(solution)/shard_map/reshape | solution.py:327
  24.2 10.6 %lags.1 = (f32[32,16,128]{2,1,0:T(8,128)S(1)}, f32[8,4,256]{2,1,0:T(4,128)S(1)}) custom-call(s32[1]{0:T(128)S(6)} %copy.10.half_ref, f32[2,32,24,128]{3,2,1,0:T(8,128)S(1)} %reshape.25.pair_ref, f32[4,16,128]{2,1,0:T(8,128)S(1)} %tile.9.model_ref, s32[4,128]{1,0:T(4,128)S(1)} %tile.21.knot_ref), custom_call_target="tpu_custom_call" | custom-call | tf_op jit(solution)/shard_map/lags/pallas_call | solution.py:334
  34.8 0.0 copy-start
  34.8 0.6 %copy-done = f32[8,4,256]{2,1,0:T(4,128)} copy-done((f32[8,4,256]{2,1,0:T(4,128)}, f32[8,4,256]{2,1,0:T(4,128)S(1)}, u32[]{:S(2)}) %copy-start) | copy-done | bytes 32792
  35.4 0.4 reshape.26
  35.9 0.6 %copy.8 = f32[4,16,32,32]{3,2,1,0:T(8,128)S(1)} copy(f32[4,16,32,32]{2,0,1,3:T(4,128)S(1)} %bitcast.11) | data formatting | bytes 524288 | tf_op jit(solution)/shard_map/transpose | solution.py:358
  36.5 1.2 %reshape.27 = f32[4,16,1024]{2,1,0:T(8,128)} reshape(f32[4,16,32,32]{3,2,1,0:T(8,128)S(1)} %copy.8) | data formatting | bytes 524288 | tf_op jit(solution)/shard_map/reshape | solution.py:358
  37.7 10.6 %owners.1 = f32[4,4,32]{2,1,0:T(4,128)} custom-call(f32[8,4,256]{2,1,0:T(4,128)} %copy-done), custom_call_target="tpu_custom_call" | custom-call | tf_op jit(solution)/shard_map/owners/pallas_call | solution.py:360
  48.3 1.3 %copy.11 = f32[4,4,32]{2,1,0:T(4,128)} copy(f32[4,4,32]{2,1,0:T(4,128)} %owners.1) | data formatting | bytes 4096
Async XLA Ops:
  1.8 8.5 %collective-permute-start = (f32[2,4,3,1024]{3,2,1,0:T(4,128)S(1)}, f32[2,4,3,1024]{3,2,1,0:T(4,128)S(1)}, u32[]{:S(2)}, u32[]{:S(2)}) collective-permute-start(f32[2,4,3,1024]{3,2,1,0:T(4,128)S(1)} %get-tuple-element.6), channel_id=1, source_target_pairs={{0,1},{1,2},{2,3},{3,4},{4,5},{5,6},{6,7},{8,9},{9,10},{10,11},{11... | collective-permute-start | bytes 294920 | tf_op jit(solution)/shard_map/ppermute | solution.py:311
  6.7 6.9 %collective-permute-start.1 = (f32[2,4,3,1024]{3,2,1,0:T(4,128)S(1)}, f32[2,4,3,1024]{3,2,1,0:T(4,128)S(1)}, u32[]{:S(2)}, u32[]{:S(2)}) collective-permute-start(f32[2,4,3,1024]{3,2,1,0:T(4,128)S(1)} %get-tuple-element.7), channel_id=1, source_target_pairs={{1,0},{2,1},{3,2},{4,3},{5,4},{6,5},{7,6},{9,8},{10,9},{11,10},{12... | collective-permute-start | bytes 294920 | tf_op jit(solution)/shard_map/ppermute | solution.py:314
  34.8 0.6 %copy-start = (f32[8,4,256]{2,1,0:T(4,128)}, f32[8,4,256]{2,1,0:T(4,128)S(1)}, u32[]{:S(2)}) copy-start(f32[8,4,256]{2,1,0:T(4,128)S(1)} %get-tuple-element.5.mine_ref) | copy-start | bytes 98308

commit v2 on v1

--- a/solution.py
+++ b/solution.py
@@ -90,27 +90,147 @@
                 put(number * SUB + j, tail[j] + run)
 
 
+def trace_rows(i, x, width):
+    return pl.ds((i * (width // SUB) + x // SUB) * SUB * SUB + x % SUB, SUB, stride=SUB)
+
+
+def edge_tile(which, j, i, lines):
+    return pl.ds(((which * HMAX + j) * lines + i) * SUB, SUB)
+
+
+def swap_blocks(parts):
+    block = lax.broadcasted_iota(jnp.int32, parts[0].shape, 1) // WINLEN
+    low, even = block < 2, block % 2 == 0
+    w, x, y, z = parts
+    w, y = jnp.where(low, w, pltpu.roll(y, 64, 1)), jnp.where(low, pltpu.roll(w, 64, 1), y)
+    x, z = jnp.where(low, x, pltpu.roll(z, 64, 1)), jnp.where(low, pltpu.roll(x, 64, 1), z)
+    w, x = jnp.where(even, w, pltpu.roll(x, 32, 1)), jnp.where(even, pltpu.roll(w, 96, 1), x)
+    y, z = jnp.where(even, y, pltpu.roll(z, 32, 1)), jnp.where(even, pltpu.roll(y, 96, 1), z)
+    return [w, x, y, z]
+
+
+def halo_kernel(width, base_ref, moni_ref, out_ref, edge, held, send_sem, recv_sem):
+    row, col = lax.axis_index("inl"), lax.axis_index("xl")
+    last = lax.axis_size("xl") - 1
+    lines = base_ref.shape[0] // (width * SUB)
+    barrier = pltpu.get_barrier_semaphore()
+    has_left, has_right = col > 0, col < last
+
+    @pl.when(has_left)
+    def _():
+        pl.semaphore_signal(barrier, inc=1, device_id=(row, col - 1), device_id_type=MESH_ID)
+
+    @pl.when(has_right)
+    def _():
+        pl.semaphore_signal(barrier, inc=1, device_id=(row, col + 1), device_id_type=MESH_ID)
+
+    for side, first in ((0, width - HMAX), (1, 0)):
+        for which, ref in enumerate((base_ref, moni_ref)):
+            for j in range(HMAX):
+                for i in range(lines):
+                    value = ref[trace_rows(i, first + j, width), :]
+                    edge[side, edge_tile(which, j, i, lines), :] = value
+
+    @pl.when(jnp.logical_and(has_left, has_right))
+    def _():
+        pl.semaphore_wait(barrier, 2)
+
+    @pl.when(jnp.logical_not(jnp.logical_and(has_left, has_right)))
+    def _():
+        pl.semaphore_wait(barrier, 1)
+
+    def copy(side, target):
+        return pltpu.make_async_remote_copy(
+            src_ref=edge.at[side],
+            dst_ref=held.at[side],
+            send_sem=send_sem.at[side],
+            recv_sem=recv_sem.at[side],
+            device_id=(row, target),
+            device_id_type=MESH_ID,
+        )
+
+    @pl.when(has_right)
+    def _():
+        copy(0, col + 1).start()
+
+    @pl.when(has_left)
+    def _():
+        copy(1, col - 1).start()
+
+    @pl.when(has_left)
+    def _():
+        pltpu.make_async_copy(edge.at[0], held.at[0], recv_sem.at[0]).wait()
+        out_ref[0] = held[0]
+
+    @pl.when(jnp.logical_not(has_left))
+    def _():
+        out_ref[0] = jnp.zeros(out_ref.shape[1:], jnp.float32)
+
+    @pl.when(has_right)
+    def _():
+        pltpu.make_async_copy(edge.at[1], held.at[1], recv_sem.at[1]).wait()
+        out_ref[1] = held[1]
+
+    @pl.when(jnp.logical_not(has_right))
+    def _():
+        out_ref[1] = jnp.zeros(out_ref.shape[1:], jnp.float32)
+
+    @pl.when(has_right)
+    def _():
+        copy(0, col + 1).wait_send()
+
+    @pl.when(has_left)
+    def _():
+        copy(1, col - 1).wait_send()
+
+
 def main_kernel(
-    half_ref, pair_ref, model_ref, knot_ref, shift_ref, normal_ref,
-    base, moni, timed, ebase, emoni, texp, tshift, tcorr, phi, flat,
+    half_ref, base_ref, moni_ref, halo_ref, coef_ref, knot_ref, shift_ref, normal_ref,
+    stage, base, moni, timed, ebase, emoni, texp, tshift, tcorr, phi, model, flat,
 ):
     width = ebase.shape[1]
     rows = base.shape[1]
+    lines = base_ref.shape[0] // (width * SUB)
     half = half_ref[0]
     take_two = (half >= 2).astype(jnp.float32)
     take_three = (half >= 3).astype(jnp.float32)
-    lane = lax.broadcasted_iota(jnp.int32, (rows, LANES), 1) % WINLEN
-    has_before = (lane != 0).astype(jnp.float32)
-    has_after = (lane != WINLEN - 1).astype(jnp.float32)
-
-    for which, (ref, halo) in enumerate(((base, TWIN), (moni, REACH))):
+    lane = lax.broadcasted_iota(jnp.int32, (SUB, LANES), 1)
+    block, tile = lane // WINLEN, lane % SUB
+    not_first, not_last = block > 0, block < 3
+    has_before, has_after = (tile > 0).astype(jnp.float32), (tile < SUB - 1).astype(jnp.float32)
+
+    def trace_tile(which, ref, i, x):
+        if x < HMAX:
+            return halo_ref[0, edge_tile(which, x, i, lines), :]
+        if x < HMAX + width:
+            return ref[trace_rows(i, x - HMAX, width), :]
+        if x < 2 * HMAX + width:
+            return halo_ref[1, edge_tile(which, x - HMAX - width, i, lines), :]
+        return jnp.zeros((SUB, LANES), jnp.float32)
+
+    for which, (ref, wide, halo) in enumerate(((base_ref, base, TWIN), (moni_ref, moni, REACH))):
+        for group in range(rows // 4):
+            parts = [
+                jnp.concatenate(
+                    [trace_tile(which, ref, i, 4 * group + m) for i in range(lines)], axis=0
+                )
+                for m in range(4)
+            ]
+            turned = jnp.concatenate(swap_blocks(parts), axis=0).T
+            stage[which, pl.ds(group * LANES, LANES), :] = turned
         for u in range(WINLEN):
-            value = pair_ref[which, u]
-            ref[halo + u] = value
-            if u >= WINLEN - halo:
-                ref[halo + u - WINLEN] = pltpu.roll(value, 1, 1) * has_before
-            if u < halo:
-                ref[halo + u + WINLEN] = pltpu.roll(value, LANES - 1, 1) * has_after
+            for part in range(rows // SUB):
+                band = pl.ds(part * SUB, SUB)
+                value = stage[which, pl.ds(part * SUB * WINLEN + u, SUB, stride=WINLEN), :]
+                wide[halo + u, band, :] = value
+                if u >= WINLEN - halo:
+                    wide[halo + u - WINLEN, band, :] = jnp.where(
+                        not_first, pltpu.roll(value, 32, 1), pltpu.roll(value, 33, 1) * has_before
+                    )
+                if u < halo:
+                    wide[halo + u + WINLEN, band, :] = jnp.where(
+                        not_last, pltpu.roll(value, 96, 1), pltpu.roll(value, 95, 1) * has_after
+                    )
 
     def smooth(term, count, put):
         for part in range(rows // SUB):
@@ -168,9 +288,21 @@
         smooth(product, WINLEN, finish)
 
     sample = lax.broadcasted_iota(jnp.int32, (WINLEN, LANES), 0).astype(jnp.float32)
+    windows = knot_ref.shape[1]
+    window = lax.broadcasted_iota(jnp.int32, (windows, LANES), 0)
+    column = lax.broadcasted_iota(jnp.int32, (windows, LANES), 1)
+    pick = (window == 4 * (column % SUB) + column // WINLEN).astype(jnp.float32)
+
+    def spread(values):
+        return lax.dot_general(
+            values, pick, (((1,), (0,)), ((), ())),
+            precision=lax.Precision.HIGHEST, preferred_element_type=jnp.float32,
+        )
+
+    starts = spread(knot_ref[...].astype(jnp.float32))
     for k in range(KW):
-        start = knot_ref[pl.ds(k, 1), :].astype(jnp.float32)
-        phi[k] = spline((sample - start) / KSTEP)
+        phi[k] = spline((sample - starts[k : k + 1]) / KSTEP)
+        model[k] = spread(coef_ref[k])
 
     for part in range(width // SUB):
         band = pl.ds(part * SUB, SUB)
@@ -178,12 +310,12 @@
         for u in range(WINLEN):
             inverse = 1.0 / texp[u, band, :]
             observed = tshift[u, band, :] * inverse
-            shift_ref[u, band, :] = observed
+            stage[0, pl.ds(part * SUB * WINLEN + u, SUB, stride=WINLEN), :] = observed
             conf = 0.5 + 0.5 * (tcorr[u, band, :] * inverse)
             basis = [phi[k, pl.ds(u, 1), :] for k in range(KW)]
-            tau = model_ref[0, band, :] * basis[0]
+            tau = model[0, band, :] * basis[0]
             for k in range(1, KW):
-                tau = tau + model_ref[k, band, :] * basis[k]
+                tau = tau + model[k, band, :] * basis[k]
             weighted = conf * (observed - tau)
             for k in range(KW):
                 sums[k] = sums[k] + weighted * basis[k]
@@ -191,8 +323,8 @@
                 sums[KW + place] = sums[KW + place] + conf * (basis[k] * basis[j])
         for place in range(TERMS):
             value = sums[place]
-            value = value + pltpu.roll(value, 2 * WINLEN, 1)
-            value = value + pltpu.roll(value, WINLEN, 1)
+            value = value + pltpu.roll(value, LANES - SUB, 1)
+            value = value + pltpu.roll(value, LANES - 2 * SUB, 1)
             flat[pl.ds(place * width + part * SUB, SUB), :] = value
     spare = flat.shape[0] - TERMS * width
     if spare:
@@ -200,7 +332,16 @@
     turned = flat[...].T
     owners, share = normal_ref.shape[0], normal_ref.shape[1]
     for owner in range(owners):
-        normal_ref[owner] = turned[owner * share : (owner + 1) * share]
+        for j in range(share):
+            window = owner * share + j
+            place = (window % 4) * WINLEN + window // 4
+            normal_ref[owner, j : j + 1] = turned[place : place + 1]
+    for group in range(width // 4):
+        back = stage[0, pl.ds(group * LANES, LANES), :].T
+        parts = swap_blocks([back[WINLEN * m : WINLEN * (m + 1)] for m in range(4)])
+        for m in range(4):
+            for i in range(lines):
+                shift_ref[trace_rows(i, 4 * group + m, width), :] = parts[m][SUB * i : SUB * (i + 1)]
 
 
 def solve_small(matrix, target):
@@ -281,20 +422,25 @@
         pltpu.make_async_copy(mine_ref.at[0], held.at[step], recv_sem.at[step]).wait()
 
     share = held.shape[1]
+    totals = []
     for part in range(each):
         total = held[part]
         for group in range(1, groups):
             total = total + held[group * each + part]
-
-        def term(number):
-            return total[:, number * width : (number + 1) * width]
-
-        matrix = [[None] * KW for _ in range(KW)]
-        for number, (k, j) in enumerate(PAIRS):
-            matrix[k][j] = term(KW + number) + (damping if k == j else 0.0)
-        delta = solve_small(matrix, [term(k) for k in range(KW)])
-        for k in range(KW):
-            out_ref[k, :, pl.ds(part * width, width)] = delta[k]
+        totals.append(total)
+    total = jnp.concatenate(totals, axis=0)
+
+    def term(number):
+        return total[:, number * width : (number + 1) * width]
+
+    matrix = [[None] * KW for _ in range(KW)]
+    for number, (k, j) in enumerate(PAIRS):
+        matrix[k][j] = term(KW + number) + (damping if k == j else 0.0)
+    delta = solve_small(matrix, [term(k) for k in range(KW)])
+    for k in range(KW):
+        for part in range(each):
+            value = delta[k][part * share : (part + 1) * share]
+            out_ref[k, :, pl.ds(part * width, width)] = value
 
     for step in range(slabs):
         self_copy = jnp.logical_and(target_row == row, col == step)
@@ -304,42 +450,53 @@
             send(step).wait_send()
 
 
-def extended(block, axis, dim, width):
-    count = lax.axis_size(axis)
-    forward = [(i, i + 1) for i in range(count - 1)]
-    backward = [(target, source) for source, target in forward]
-    low = lax.ppermute(
-        lax.slice_in_dim(block, block.shape[dim] - width, None, axis=dim), axis, forward
-    )
-    high = lax.ppermute(lax.slice_in_dim(block, 0, width, axis=dim), axis, backward)
-    return jnp.concatenate([low, block, high], axis=dim)
+def as_rows(block):
+    lines, width, samples = block.shape
+    tiles = block.reshape(lines, width // SUB, SUB, samples // LANES, LANES)
+    return tiles.transpose(0, 1, 3, 2, 4).reshape(-1, LANES)
+
+
+def from_rows(flat, lines, width, samples):
+    tiles = flat.reshape(lines, width // SUB, samples // LANES, SUB, LANES)
+    return tiles.transpose(0, 1, 3, 2, 4).reshape(lines, width, samples)
 
 
 def per_device(baseline, monitor, shift_model, knot_start, half_width):
-    inline_rows, width, samples = baseline.shape
+    lines, width, samples = baseline.shape
     windows = samples // WINLEN
     groups, slabs = lax.axis_size("inl"), lax.axis_size("xl")
-    share = windows // slabs
+    share, each = windows // slabs, slabs // groups
     rows = -(-(width + 2 * HMAX) // SUB) * SUB
-    paired = extended(jnp.stack([baseline, monitor]), "xl", 2, HMAX)
-    paired = jnp.pad(paired, ((0, 0), (0, 0), (0, rows - width - 2 * HMAX), (0, 0)))
-    pair = paired.reshape(2, inline_rows, rows, windows, WINLEN)
-    pair = pair.transpose(0, 4, 2, 1, 3).reshape(2, WINLEN, rows, LANES)
-    model = jnp.tile(shift_model.transpose(0, 2, 1), (1, 1, inline_rows))
-    knots = jnp.tile(knot_start.T, (1, inline_rows))
     packed = -(-(TERMS * width) // LANES) * LANES
     block = (WINLEN, width, LANES)
     f32 = jnp.float32
     whole = pl.BlockSpec(memory_space=pltpu.VMEM)
+    base_rows, moni_rows = as_rows(baseline), as_rows(monitor)
+    edges = (2, 2 * HMAX * lines * SUB, LANES)
+    halo = pl.pallas_call(
+        functools.partial(halo_kernel, width),
+        out_shape=jax.ShapeDtypeStruct(edges, f32),
+        in_specs=[whole, whole],
+        out_specs=whole,
+        scratch_shapes=[
+            pltpu.VMEM(edges, f32),
+            pltpu.VMEM(edges, f32),
+            pltpu.SemaphoreType.DMA((2,)),
+            pltpu.SemaphoreType.DMA((2,)),
+        ],
+        compiler_params=pltpu.CompilerParams(collective_id=1, has_side_effects=True),
+        name="halo",
+    )(base_rows, moni_rows)
     shift, normal = pl.pallas_call(
         main_kernel,
         out_shape=(
-            jax.ShapeDtypeStruct(block, f32),
+            jax.ShapeDtypeStruct(base_rows.shape, f32),
             jax.ShapeDtypeStruct((slabs, share, packed), f32),
         ),
-        in_specs=[pl.BlockSpec(memory_space=pltpu.SMEM), whole, whole, whole],
+        in_specs=[pl.BlockSpec(memory_space=pltpu.SMEM)] + [whole] * 5,
         out_specs=(whole, whole),
         scratch_shapes=[
+            pltpu.VMEM((2, rows * WINLEN, LANES), f32),
             pltpu.VMEM((WINLEN + 2 * TWIN, rows, LANES), f32),
             pltpu.VMEM((WINLEN + 2 * REACH + 2, rows, LANES), f32),
             pltpu.VMEM((WINLEN + 2 * LAGS, rows, LANES), f32),
@@ -349,16 +506,15 @@
             pltpu.VMEM(block, f32),
             pltpu.VMEM(block, f32),
             pltpu.VMEM((KW, WINLEN, LANES), f32),
+            pltpu.VMEM((KW, width, LANES), f32),
             pltpu.VMEM((packed, LANES), f32),
         ],
         compiler_params=pltpu.CompilerParams(vmem_limit_bytes=32 * 1024 * 1024),
         name="lags",
-    )(half_width, pair, model, knots)
-    shift_obs = shift.reshape(WINLEN, width, inline_rows, windows)
-    shift_obs = shift_obs.transpose(2, 1, 3, 0).reshape(inline_rows, width, samples)
-    each = slabs // groups
+    )(half_width, base_rows, moni_rows, halo, shift_model.transpose(0, 2, 1), knot_start.T)
+    shift_obs = from_rows(shift, lines, width, samples)
     delta = pl.pallas_call(
-        functools.partial(owner_kernel, groups, slabs, width, DAMPING * inline_rows * groups),
+        functools.partial(owner_kernel, groups, slabs, width, DAMPING * lines * groups),
         out_shape=jax.ShapeDtypeStruct((KW, share, each * width), f32),
         in_specs=[whole],
         out_specs=whole,

time: 50 us -> 38.2 us (0.76)
  Pallas kernels: 21.2 us -> 33.7 us
  local copies, waits for them, and re-layouts: 14.4 us -> 2.84 us
  starting transfers between devices: 6.17 us -> 0 us
  other arithmetic: 3.23 us -> 0 us
  waiting for transfers between devices: 3.22 us -> 0 us
    pallas_call x1 -> x2, Pallas kernels: 10.6 us -> 22.7 us  [the longest x1 13.7 us: per_device(): pl.pallas_call(main_kernel, out_shape=(jax.ShapeDtypeStruct(base_rows.sha...]
    reshape x5 -> x0, local copies, waits for them, and re-layouts: 10.2 us -> none  [the longest x2 5.73 us: per_device(): pair = paired.reshape(2, inline_rows, rows, windows, WINLEN)]
    ppermute x2 -> x0, starting transfers between devices: 6.17 us -> none  [the longest x1 4.88 us: extended(): lax.ppermute(lax.slice_in_dim(block, block.shape[dim] - width, None, axis...]
    ppermute x2 -> x0, waiting for transfers between devices: 3.22 us -> none  [the longest x1 3.22 us: extended(): lax.ppermute(lax.slice_in_dim(block, 0, width, axis=dim), axis, backward)]
    concatenate x1 -> x0, other arithmetic: 2.08 us -> none  [extended(): return jnp.concatenate([low, block, high], axis=dim)]
    another operation x4 -> x0, local copies, waits for them, and re-layouts: 1.67 us -> none  [the longest x2 0.9 us: per_device(): model = jnp.tile(shift_model.transpose(0, 2, 1), (1, 1, inline_rows))]
    slice x1 -> x0, other arithmetic: 1.15 us -> none  [extended(): lax.slice_in_dim(block, block.shape[dim] - width, None, axis=dim)]
    unnamed x3 -> x13, local copies, waits for them, and re-layouts: 1.93 us -> 2.84 us
  transfers between devices with their start and end apart: 2 -> 0, of which waited for: 1 -> 0; matrix products, arithmetic and copies ran while one was open for 3% -> 0% of each run, Pallas kernels for 0% -> 0%
where the time goes in v2:
time: 38.2 us; the launch traced here: 37.9 us
  Pallas kernels  33.7 us (88%)
  local copies, waits for them, and re-layouts  2.84 us (7%)
  between operations  1.37 us (4%)
    pallas_call x1, Pallas kernels, per_device(): pl.pallas_call(main_kernel, out_shape=(jax.ShapeDtypeStruct(base_rows.sha...  13.7 us
    pallas_call x1, Pallas kernels, per_device(): pl.pallas_call(functools.partial(owner_kernel, groups, slabs, width, DAMP...  11.1 us
    pallas_call x1, Pallas kernels, per_device(): pl.pallas_call(functools.partial(halo_kernel, width), out_shape=jax.Shape...  8.92 us
    unnamed x13, local copies, waits for them, and re-layouts  2.84 us

profile of v2, /device:TPU:0, one launch (start us, length us, event | category | flops | bytes accessed | tf_op | source)
XLA Modules:
  0.0 37.9 jit_solution(276289034192864340)
XLA Ops:
  1.3 0.0 copy-start
  1.3 0.0 copy-start.1
  1.3 0.0 copy-start.3
  1.3 0.0 copy-start.5
  1.3 8.9 %halo.1.halo_ref = f32[2,192,128]{2,1,0:T(8,128)} custom-call(f32[512,128]{1,0:T(8,128)} %bitcast.17, f32[512,128]{1,0:T(8,128)} %bitcast.19), custom_call_target="tpu_custom_call" | custom-call | tf_op jit(solution)/shard_map/halo/pallas_call | solution.py:476
  10.2 0.0 copy-done
  10.3 0.0 copy-done.1
  10.3 0.0 copy-done.3
  10.3 0.0 copy-done.5
  10.3 0.0 copy-start.2
  10.3 0.9 %copy-done.2 = f32[2,192,128]{2,1,0:T(8,128)S(1)} copy-done((f32[2,192,128]{2,1,0:T(8,128)S(1)}, f32[2,192,128]{2,1,0:T(8,128)}, u32[]{:S(2)}) %copy-start.2) | copy-done | bytes 196632
  11.2 13.7 %lags.1 = (f32[512,128]{1,0:T(8,128)}, f32[8,4,256]{2,1,0:T(4,128)S(1)}) custom-call(s32[1]{0:T(128)S(6)} %copy.8.half_ref, f32[512,128]{1,0:T(8,128)S(1)} %bitcast.18, f32[512,128]{1,0:T(8,128)S(1)} %bitcast.20, f32[2,192,128]{2,1,0:T(8,128)S(1)} %copy-done.2, f32[4,16,32]{2,1,0:T(8,128)S(1)} %bitcast.21, s32[4,32]{1,0:T(4,128)S(1)} %bitcast.22), custom_call_target="tpu_custom_call" | custom-call | tf_op jit(solution)/shard_map/lags/pallas_call | solution.py:490
  24.9 0.0 copy-start.4
  25.0 0.6 %copy-done.4 = f32[8,4,256]{2,1,0:T(4,128)} copy-done((f32[8,4,256]{2,1,0:T(4,128)}, f32[8,4,256]{2,1,0:T(4,128)S(1)}, u32[]{:S(2)}) %copy-start.4) | copy-done | bytes 32792
  25.6 11.1 %owners.1 = f32[4,4,32]{2,1,0:T(4,128)} custom-call(f32[8,4,256]{2,1,0:T(4,128)} %copy-done.4), custom_call_target="tpu_custom_call" | custom-call | tf_op jit(solution)/shard_map/owners/pallas_call | solution.py:516
  36.6 1.3 %copy.9 = f32[4,4,32]{2,1,0:T(4,128)} copy(f32[4,4,32]{2,1,0:T(4,128)} %owners.1) | data formatting | bytes 4096
Async XLA Ops:
  1.3 9.0 %copy-start = (f32[4,16,1024]{2,1,0:T(8,128)S(1)}, f32[4,16,1024]{2,1,0:T(8,128)}, u32[]{:S(2)}) copy-start(f32[4,16,1024]{2,1,0:T(8,128)} %param.5) | copy-start | bytes 786436
  1.3 9.0 %copy-start.1 = (f32[4,16,1024]{2,1,0:T(8,128)S(1)}, f32[4,16,1024]{2,1,0:T(8,128)}, u32[]{:S(2)}) copy-start(f32[4,16,1024]{2,1,0:T(8,128)} %param.6) | copy-start | bytes 786436
  1.3 9.0 %copy-start.3 = (f32[4,32,16]{1,2,0:T(8,128)S(1)}, f32[4,32,16]{1,2,0:T(8,128)}, u32[]{:S(2)}) copy-start(f32[4,32,16]{1,2,0:T(8,128)} %param.7) | copy-start | bytes 24580
  1.3 9.0 %copy-start.5 = (s32[32,4]{0,1:T(4,128)S(1)}, s32[32,4]{0,1:T(4,128)}, u32[]{:S(2)}) copy-start(s32[32,4]{0,1:T(4,128)} %param.8) | copy-start | bytes 1540
  10.3 0.9 %copy-start.2 = (f32[2,192,128]{2,1,0:T(8,128)S(1)}, f32[2,192,128]{2,1,0:T(8,128)}, u32[]{:S(2)}) copy-start(f32[2,192,128]{2,1,0:T(8,128)} %halo.1.halo_ref) | copy-start | bytes 589828
  24.9 0.6 %copy-start.4 = (f32[8,4,256]{2,1,0:T(4,128)}, f32[8,4,256]{2,1,0:T(4,128)S(1)}, u32[]{:S(2)}) copy-start(f32[8,4,256]{2,1,0:T(4,128)S(1)} %get-tuple-element.5.mine_ref) | copy-start | bytes 98308

commit v3 on v2

--- a/solution.py
+++ b/solution.py
@@ -484,7 +484,7 @@
             pltpu.SemaphoreType.DMA((2,)),
             pltpu.SemaphoreType.DMA((2,)),
         ],
-        compiler_params=pltpu.CompilerParams(collective_id=1, has_side_effects=True),
+        compiler_params=pltpu.CompilerParams(collective_id=1, has_side_effects=True, vmem_limit_bytes=8 * 1024 * 1024),
         name="halo",
     )(base_rows, moni_rows)
     shift, normal = pl.pallas_call(
@@ -523,7 +523,7 @@
             pltpu.SemaphoreType.DMA((slabs,)),
             pltpu.SemaphoreType.DMA((slabs,)),
         ],
-        compiler_params=pltpu.CompilerParams(collective_id=0, has_side_effects=True),
+        compiler_params=pltpu.CompilerParams(collective_id=0, has_side_effects=True, vmem_limit_bytes=8 * 1024 * 1024),
         name="owners",
     )(normal)
     return (shift_obs, delta)

time: 38.2 us -> 34.4 us (0.901)
  Pallas kernels: 33.7 us -> 30.4 us
    pallas_call x1, Pallas kernels: 8.92 us -> 7.2 us  [per_device(): pl.pallas_call(functools.partial(halo_kernel, width), out_shape=jax.Shape...]
    pallas_call x1, Pallas kernels: 11.1 us -> 9.71 us  [per_device(): pl.pallas_call(functools.partial(owner_kernel, groups, slabs, width, DAMP...]
where the time goes in v3:
time: 34.4 us; the launch traced here: 34.2 us
  Pallas kernels  30.4 us (88%)
  local copies, waits for them, and re-layouts  2.51 us (7%)
  between operations  1.34 us (4%)
    pallas_call x1, Pallas kernels, per_device(): pl.pallas_call(main_kernel, out_shape=(jax.ShapeDtypeStruct(base_rows.sha...  13.5 us
    pallas_call x1, Pallas kernels, per_device(): pl.pallas_call(functools.partial(owner_kernel, groups, slabs, width, DAMP...  9.71 us
    pallas_call x1, Pallas kernels, per_device(): pl.pallas_call(functools.partial(halo_kernel, width), out_shape=jax.Shape...  7.2 us
    unnamed x13, local copies, waits for them, and re-layouts  2.51 us

profile of v3, /device:TPU:0, one launch (start us, length us, event | category | flops | bytes accessed | tf_op | source)
XLA Modules:
  0.0 34.2 jit_solution(14846386241418646435)
XLA Ops:
  1.3 0.0 copy-start
  1.3 0.9 %copy-done = f32[4,16,1024]{2,1,0:T(8,128)S(1)} copy-done((f32[4,16,1024]{2,1,0:T(8,128)S(1)}, f32[4,16,1024]{2,1,0:T(8,128)}, u32[]{:S(2)}) %copy-start) | copy-done | bytes 262168
  2.2 0.0 copy-start.2
  2.2 0.9 %copy-done.2 = f32[4,16,1024]{2,1,0:T(8,128)S(1)} copy-done((f32[4,16,1024]{2,1,0:T(8,128)S(1)}, f32[4,16,1024]{2,1,0:T(8,128)}, u32[]{:S(2)}) %copy-start.2) | copy-done | bytes 262168
  3.2 0.0 copy-start.1
  3.2 0.0 copy-start.3
  3.2 0.0 copy-start.4
  3.2 0.0 copy-start.5
  3.2 7.2 %halo.1.halo_ref = f32[2,192,128]{2,1,0:T(8,128)S(1)} custom-call(f32[512,128]{1,0:T(8,128)S(1)} %bitcast.17, f32[512,128]{1,0:T(8,128)S(1)} %bitcast.19), custom_call_target="tpu_custom_call" | custom-call | tf_op jit(solution)/shard_map/halo/pallas_call | solution.py:476
  10.4 0.0 copy-done.1
  10.4 0.0 copy-done.3
  10.4 0.0 copy-done.4
  10.4 0.0 copy-done.5
  10.4 13.5 %lags.1 = (f32[512,128]{1,0:T(8,128)}, f32[8,4,256]{2,1,0:T(4,128)S(1)}) custom-call(s32[1]{0:T(128)S(6)} %copy.8.half_ref, f32[512,128]{1,0:T(8,128)S(1)} %bitcast.18, f32[512,128]{1,0:T(8,128)S(1)} %bitcast.20, f32[2,192,128]{2,1,0:T(8,128)S(1)} %halo.1.halo_ref, f32[4,16,32]{2,1,0:T(8,128)S(1)} %bitcast.21, s32[4,32]{1,0:T(4,128)S(1)} %bitcast.22), custom_call_target="tpu_custom_call" | custom-call | tf_op jit(solution)/shard_map/lags/pallas_call | solution.py:490
  23.9 9.7 %owners.1 = f32[4,4,32]{2,1,0:T(4,128)S(1)} custom-call(f32[8,4,256]{2,1,0:T(4,128)S(1)} %get-tuple-element.5.mine_ref), custom_call_target="tpu_custom_call" | custom-call | tf_op jit(solution)/shard_map/owners/pallas_call | solution.py:516
  33.6 0.6 %copy.9 = f32[4,4,32]{2,1,0:T(4,128)} copy(f32[4,4,32]{2,1,0:T(4,128)S(1)} %owners.1) | data formatting | bytes 4096
Async XLA Ops:
  1.3 1.0 %copy-start = (f32[4,16,1024]{2,1,0:T(8,128)S(1)}, f32[4,16,1024]{2,1,0:T(8,128)}, u32[]{:S(2)}) copy-start(f32[4,16,1024]{2,1,0:T(8,128)} %param.5) | copy-start | bytes 786436
  2.2 0.9 %copy-start.2 = (f32[4,16,1024]{2,1,0:T(8,128)S(1)}, f32[4,16,1024]{2,1,0:T(8,128)}, u32[]{:S(2)}) copy-start(f32[4,16,1024]{2,1,0:T(8,128)} %param.6) | copy-start | bytes 786436
  3.2 7.2 %copy-start.1 = (f32[4,16,1024]{2,1,0:T(8,128)S(1)}, f32[4,16,1024]{2,1,0:T(8,128)}, u32[]{:S(2)}) copy-start(f32[4,16,1024]{2,1,0:T(8,128)} %param.5) | copy-start | bytes 786436
  3.2 7.2 %copy-start.3 = (f32[4,16,1024]{2,1,0:T(8,128)S(1)}, f32[4,16,1024]{2,1,0:T(8,128)}, u32[]{:S(2)}) copy-start(f32[4,16,1024]{2,1,0:T(8,128)} %param.6) | copy-start | bytes 786436
  3.2 7.2 %copy-start.4 = (f32[4,32,16]{1,2,0:T(8,128)S(1)}, f32[4,32,16]{1,2,0:T(8,128)}, u32[]{:S(2)}) copy-start(f32[4,32,16]{1,2,0:T(8,128)} %param.7) | copy-start | bytes 24580
  3.2 7.2 %copy-start.5 = (s32[32,4]{0,1:T(4,128)S(1)}, s32[32,4]{0,1:T(4,128)}, u32[]{:S(2)}) copy-start(s32[32,4]{0,1:T(4,128)} %param.8) | copy-start | bytes 1540
